TPU v7x, 32 devices: a whole 2x2x4 slice. The times are simulated.
32 devices in a mesh: dp: 4 (over y, x), fsdp: 8 (over z, core).
Axes of the slice: x: 2, y: 2, z: 4, core: 2. Of those that a mesh axis runs over, the one named last changes fastest.
Arguments:
- tokens: bfloat16 [32, 512, 768], P(('dp', 'fsdp')), may hold values from -6 to 6
- lengths: int32 [32], P(('dp', 'fsdp')), may hold values from 30 to 512, as said below
- cotangent: bfloat16 [32, 512, 768], P(('dp', 'fsdp')), may hold values from -6 to 6
- query_weight: bfloat16 [768, 768], P('fsdp'), may hold values from -0.21875 to 0.21875
- query_bias: bfloat16 [768], P('fsdp'), may hold values from -3 to 3
- key_weight: bfloat16 [768, 768], P('fsdp'), may hold values from -0.21875 to 0.21875
- value_weight: bfloat16 [768, 768], P('fsdp'), may hold values from -0.21875 to 0.21875
- value_bias: bfloat16 [768], P('fsdp'), may hold values from -3 to 3
- output_weight: bfloat16 [768, 768], P('fsdp'), may hold values from -3.5 to 3.5
- output_bias: bfloat16 [768], P('fsdp'), may hold values from -3 to 3
- first_gain: bfloat16 [768], P('fsdp'), may hold values from 0.25 to 1.75
- first_shift: bfloat16 [768], P('fsdp'), may hold values from -3 to 3
- inner_weight: bfloat16 [768, 3072], P('fsdp'), may hold values from -0.21875 to 0.21875
- inner_bias: bfloat16 [3072], P('fsdp'), may hold values from -3 to 3
- outer_weight: bfloat16 [3072, 768], P('fsdp'), may hold values from -0.109375 to 0.109375
- outer_bias: bfloat16 [768], P('fsdp'), may hold values from -3 to 3
- second_gain: bfloat16 [768], P('fsdp'), may hold values from 0.25 to 1.75
- second_shift: bfloat16 [768], P('fsdp'), may hold values from -3 to 3
Outputs:
- block_output: bfloat16 [32, 512, 768], P(('dp', 'fsdp'))
- input_grad: float32 [32, 512, 768], P(('dp', 'fsdp'))
- query_weight_grad: float32 [768, 768], P('fsdp')
- query_bias_grad: float32 [768], P('fsdp')
- key_weight_grad: float32 [768, 768], P('fsdp')
- value_weight_grad: float32 [768, 768], P('fsdp')
- value_bias_grad: float32 [768], P('fsdp')
- output_weight_grad: float32 [768, 768], P('fsdp')
- output_bias_grad: float32 [768], P('fsdp')
- first_gain_grad: float32 [768], P('fsdp')
- first_shift_grad: float32 [768], P('fsdp')
- inner_weight_grad: float32 [768, 3072], P('fsdp')
- inner_bias_grad: float32 [3072], P('fsdp')
- outer_weight_grad: float32 [3072, 768], P('fsdp')
- outer_bias_grad: float32 [768], P('fsdp')
- second_gain_grad: float32 [768], P('fsdp')
- second_shift_grad: float32 [768], P('fsdp')
Inputs may be any that keep to these rules, and one draw needn't show every extreme that they name: Document i holds its true tokens in slots 0 to lengths[i] - 1, the rest is padding; in every draw some document has exactly 512 and another exactly 30.
All inputs are finite; a program needn't handle non-finite values.
Results may differ from a plain program's by a relative error of at most 0.015.
Values may be sent and summed in bfloat16 or wider, within the bound.
No kernel may reach another device: no remote copies, remote signals or barrier semaphores. Data moves between devices by JAX's collectives and lax.ppermute only.
A program may use at most 192 MiB of HBM per device.

v0:
```python
import math
import jax
import jax.numpy as jnp
from jax import lax
from jax.sharding import PartitionSpec as P

HD = 64
epsilon = 1e-12
masked_score = -1e30
root_half = math.sqrt(0.5)
inv_root_two_pi = 1.0 / math.sqrt(2.0 * math.pi)


def normalize(values):
    center = values - jnp.mean(values, axis=-1, keepdims=True)
    scaled = lax.rsqrt(jnp.mean(center * center, axis=-1, keepdims=True) + epsilon)
    return (center * scaled, scaled)


def norm_back(grad_in, normed, scaled):
    first_mean = jnp.mean(grad_in, axis=-1, keepdims=True)
    second_mean = jnp.mean(grad_in * normed, axis=-1, keepdims=True)
    return scaled * (grad_in - first_mean - normed * second_mean)


def gelu_parts(inner):
    cumulative = 0.5 * (1.0 + lax.erf(inner * root_half))
    density = jnp.exp(-0.5 * inner * inner) * inv_root_two_pi
    return (inner * cumulative, cumulative + inner * density)


def score_block(queries, keysets, length):
    seq_len = queries.shape[0]
    scores = jnp.einsum(
        "qhd,khd->hqk", queries, keysets, preferred_element_type=jnp.float32
    ) * queries.shape[2] ** (-0.5)
    allowed = jnp.arange(seq_len, dtype=jnp.int32) < length
    return jnp.where(allowed[None, None, :], scores, masked_score)


def attend_forward(pieces):
    queries, keysets, values, length = pieces
    scores = score_block(queries, keysets, length)
    highest = jnp.max(scores, axis=-1, keepdims=True)
    logsum = highest + jnp.log(jnp.sum(jnp.exp(scores - highest), axis=-1, keepdims=True))
    probs = jnp.exp(scores - logsum).astype(jnp.bfloat16)
    attended = jnp.einsum("hqk,khd->qhd", probs, values, preferred_element_type=jnp.float32)
    return (attended.astype(jnp.bfloat16), logsum)


def attend_backward(pieces):
    queries, keysets, values, length, logsum, attended_grad = pieces
    scale = queries.shape[2] ** (-0.5)
    scores = score_block(queries, keysets, length)
    probs_full = jnp.exp(scores - logsum)
    probs = probs_full.astype(jnp.bfloat16)
    values_grad = jnp.einsum(
        "hqk,qhd->khd", probs, attended_grad, preferred_element_type=jnp.float32
    )
    prob_grad = jnp.einsum(
        "qhd,khd->hqk", attended_grad, values, preferred_element_type=jnp.float32
    )
    row_term = jnp.sum(prob_grad * probs_full, axis=-1, keepdims=True)
    score_grad = (probs_full * (prob_grad - row_term)).astype(jnp.bfloat16)
    queries_grad = (
        jnp.einsum("hqk,khd->qhd", score_grad, keysets, preferred_element_type=jnp.float32) * scale
    )
    keys_grad = (
        jnp.einsum("hqk,qhd->khd", score_grad, queries, preferred_element_type=jnp.float32) * scale
    )
    return (
        queries_grad.astype(jnp.bfloat16),
        keys_grad.astype(jnp.bfloat16),
        values_grad.astype(jnp.bfloat16),
    )


def column_sum(values):
    return jnp.sum(values.astype(jnp.float32), axis=0)


def weight_grad(left, right):
    return jnp.einsum("tr,tc->rc", left, right, preferred_element_type=jnp.float32)


def back_product(grad_rows, weights):
    return jnp.einsum("tc,rc->tr", grad_rows, weights, preferred_element_type=jnp.float32)


def on_device(
    tokens,
    lengths,
    cotangent,
    query_weight,
    query_bias,
    key_weight,
    value_weight,
    value_bias,
    output_weight,
    output_bias,
    first_gain,
    first_shift,
    inner_weight,
    inner_bias,
    outer_weight,
    outer_bias,
    second_gain,
    second_shift,
):
    gathered = (
        lax.all_gather(query_weight, "fsdp", axis=0, tiled=True),
        lax.all_gather(query_bias, "fsdp", axis=0, tiled=True),
        lax.all_gather(key_weight, "fsdp", axis=0, tiled=True),
        lax.all_gather(value_weight, "fsdp", axis=0, tiled=True),
        lax.all_gather(value_bias, "fsdp", axis=0, tiled=True),
        lax.all_gather(output_weight, "fsdp", axis=0, tiled=True),
        lax.all_gather(output_bias, "fsdp", axis=0, tiled=True),
        lax.all_gather(first_gain, "fsdp", axis=0, tiled=True),
        lax.all_gather(first_shift, "fsdp", axis=0, tiled=True),
        lax.all_gather(inner_weight, "fsdp", axis=0, tiled=True),
        lax.all_gather(inner_bias, "fsdp", axis=0, tiled=True),
        lax.all_gather(outer_weight, "fsdp", axis=0, tiled=True),
        lax.all_gather(outer_bias, "fsdp", axis=0, tiled=True),
        lax.all_gather(second_gain, "fsdp", axis=0, tiled=True),
        lax.all_gather(second_shift, "fsdp", axis=0, tiled=True),
    )
    (
        full_query,
        full_qbias,
        full_key,
        full_value,
        full_vbias,
        full_output,
        full_obias,
        full_gain_one,
        full_shift_one,
        full_inner,
        full_ibias,
        full_outer,
        full_ubias,
        full_gain_two,
        full_shift_two,
    ) = gathered
    doc_count, seq_len, width = tokens.shape
    row_count = doc_count * seq_len
    heads = width // HD
    flat_in = tokens.reshape(row_count, width)
    queries = (
        jnp.dot(flat_in, full_query, preferred_element_type=jnp.float32)
        + full_qbias.astype(jnp.float32)
    ).astype(jnp.bfloat16)
    keysets = jnp.dot(flat_in, full_key, preferred_element_type=jnp.float32).astype(jnp.bfloat16)
    values = (
        jnp.dot(flat_in, full_value, preferred_element_type=jnp.float32)
        + full_vbias.astype(jnp.float32)
    ).astype(jnp.bfloat16)
    shaped = (doc_count, seq_len, heads, HD)
    query_docs = queries.reshape(shaped)
    key_docs = keysets.reshape(shaped)
    value_docs = values.reshape(shaped)
    attended, logsum = lax.map(attend_forward, (query_docs, key_docs, value_docs, lengths))
    attended = attended.reshape(row_count, width)
    first_sum = (
        flat_in.astype(jnp.float32)
        + jnp.dot(attended, full_output, preferred_element_type=jnp.float32)
        + full_obias.astype(jnp.float32)
    )
    normed_one, rstd_one = normalize(first_sum)
    hidden = normed_one * full_gain_one.astype(jnp.float32) + full_shift_one.astype(jnp.float32)
    hidden_low = hidden.astype(jnp.bfloat16)
    inner = jnp.dot(hidden_low, full_inner, preferred_element_type=jnp.float32) + full_ibias.astype(
        jnp.float32
    )
    activated_full, slope = gelu_parts(inner)
    activated = activated_full.astype(jnp.bfloat16)
    second_sum = (
        hidden
        + jnp.dot(activated, full_outer, preferred_element_type=jnp.float32)
        + full_ubias.astype(jnp.float32)
    )
    normed_two, rstd_two = normalize(second_sum)
    valid = (
        (jnp.arange(seq_len, dtype=jnp.int32)[None, :] < lengths[:, None])
        .astype(jnp.float32)
        .reshape(row_count, 1)
    )
    result = valid * (
        normed_two * full_gain_two.astype(jnp.float32) + full_shift_two.astype(jnp.float32)
    )
    block_output = result.astype(jnp.bfloat16).reshape(doc_count, seq_len, width)
    again = (
        lax.all_gather(query_weight, "fsdp", axis=0, tiled=True),
        lax.all_gather(query_bias, "fsdp", axis=0, tiled=True),
        lax.all_gather(key_weight, "fsdp", axis=0, tiled=True),
        lax.all_gather(value_weight, "fsdp", axis=0, tiled=True),
        lax.all_gather(value_bias, "fsdp", axis=0, tiled=True),
        lax.all_gather(output_weight, "fsdp", axis=0, tiled=True),
        lax.all_gather(output_bias, "fsdp", axis=0, tiled=True),
        lax.all_gather(first_gain, "fsdp", axis=0, tiled=True),
        lax.all_gather(first_shift, "fsdp", axis=0, tiled=True),
        lax.all_gather(inner_weight, "fsdp", axis=0, tiled=True),
        lax.all_gather(inner_bias, "fsdp", axis=0, tiled=True),
        lax.all_gather(outer_weight, "fsdp", axis=0, tiled=True),
        lax.all_gather(outer_bias, "fsdp", axis=0, tiled=True),
        lax.all_gather(second_gain, "fsdp", axis=0, tiled=True),
        lax.all_gather(second_shift, "fsdp", axis=0, tiled=True),
    )
    back_query = again[0]
    back_key = again[2]
    back_value = again[3]
    back_output = again[5]
    back_gain_one = again[7]
    back_inner = again[9]
    back_outer = again[11]
    back_gain_two = again[13]
    out_grad = cotangent.reshape(row_count, width).astype(jnp.float32) * valid
    second_shift_grad = jnp.sum(out_grad, axis=0)
    second_gain_grad = jnp.sum(out_grad * normed_two, axis=0)
    second_sum_grad = norm_back(out_grad * back_gain_two.astype(jnp.float32), normed_two, rstd_two)
    outer_grad_low = second_sum_grad.astype(jnp.bfloat16)
    outer_bias_grad = column_sum(outer_grad_low)
    outer_weight_grad = weight_grad(activated, outer_grad_low)
    inner_grad_low = (back_product(outer_grad_low, back_outer) * slope).astype(jnp.bfloat16)
    inner_bias_grad = column_sum(inner_grad_low)
    inner_weight_grad = weight_grad(hidden_low, inner_grad_low)
    hidden_grad = back_product(inner_grad_low, back_inner) + second_sum_grad
    first_shift_grad = jnp.sum(hidden_grad, axis=0)
    first_gain_grad = jnp.sum(hidden_grad * normed_one, axis=0)
    first_sum_grad = norm_back(
        hidden_grad * back_gain_one.astype(jnp.float32), normed_one, rstd_one
    )
    branch_grad_low = first_sum_grad.astype(jnp.bfloat16)
    output_bias_grad = column_sum(branch_grad_low)
    output_weight_grad = weight_grad(attended, branch_grad_low)
    attended_grad_low = back_product(branch_grad_low, back_output).astype(jnp.bfloat16)
    queries_grad, keys_grad, values_grad = lax.map(
        attend_backward,
        (query_docs, key_docs, value_docs, lengths, logsum, attended_grad_low.reshape(shaped)),
    )
    queries_grad = queries_grad.reshape(row_count, width)
    keys_grad = keys_grad.reshape(row_count, width)
    values_grad = values_grad.reshape(row_count, width)
    query_bias_grad = column_sum(queries_grad)
    value_bias_grad = column_sum(values_grad)
    query_weight_grad = weight_grad(flat_in, queries_grad)
    key_weight_grad = weight_grad(flat_in, keys_grad)
    value_weight_grad = weight_grad(flat_in, values_grad)
    input_grad = (
        first_sum_grad
        + back_product(queries_grad, back_query)
        + back_product(keys_grad, back_key)
        + back_product(values_grad, back_value)
    )
    local_grads = (
        query_weight_grad,
        query_bias_grad,
        key_weight_grad,
        value_weight_grad,
        value_bias_grad,
        output_weight_grad,
        output_bias_grad,
        first_gain_grad,
        first_shift_grad,
        inner_weight_grad,
        inner_bias_grad,
        outer_weight_grad,
        outer_bias_grad,
        second_gain_grad,
        second_shift_grad,
    )
    owned = (
        lax.psum_scatter(local_grads[0], "fsdp", scatter_dimension=0, tiled=True),
        lax.psum_scatter(local_grads[1], "fsdp", scatter_dimension=0, tiled=True),
        lax.psum_scatter(local_grads[2], "fsdp", scatter_dimension=0, tiled=True),
        lax.psum_scatter(local_grads[3], "fsdp", scatter_dimension=0, tiled=True),
        lax.psum_scatter(local_grads[4], "fsdp", scatter_dimension=0, tiled=True),
        lax.psum_scatter(local_grads[5], "fsdp", scatter_dimension=0, tiled=True),
        lax.psum_scatter(local_grads[6], "fsdp", scatter_dimension=0, tiled=True),
        lax.psum_scatter(local_grads[7], "fsdp", scatter_dimension=0, tiled=True),
        lax.psum_scatter(local_grads[8], "fsdp", scatter_dimension=0, tiled=True),
        lax.psum_scatter(local_grads[9], "fsdp", scatter_dimension=0, tiled=True),
        lax.psum_scatter(local_grads[10], "fsdp", scatter_dimension=0, tiled=True),
        lax.psum_scatter(local_grads[11], "fsdp", scatter_dimension=0, tiled=True),
        lax.psum_scatter(local_grads[12], "fsdp", scatter_dimension=0, tiled=True),
        lax.psum_scatter(local_grads[13], "fsdp", scatter_dimension=0, tiled=True),
        lax.psum_scatter(local_grads[14], "fsdp", scatter_dimension=0, tiled=True),
    )
    summed = (
        lax.psum(owned[0].astype(jnp.bfloat16), "dp").astype(jnp.float32),
        lax.psum(owned[1].astype(jnp.bfloat16), "dp").astype(jnp.float32),
        lax.psum(owned[2].astype(jnp.bfloat16), "dp").astype(jnp.float32),
        lax.psum(owned[3].astype(jnp.bfloat16), "dp").astype(jnp.float32),
        lax.psum(owned[4].astype(jnp.bfloat16), "dp").astype(jnp.float32),
        lax.psum(owned[5].astype(jnp.bfloat16), "dp").astype(jnp.float32),
        lax.psum(owned[6].astype(jnp.bfloat16), "dp").astype(jnp.float32),
        lax.psum(owned[7].astype(jnp.bfloat16), "dp").astype(jnp.float32),
        lax.psum(owned[8].astype(jnp.bfloat16), "dp").astype(jnp.float32),
        lax.psum(owned[9].astype(jnp.bfloat16), "dp").astype(jnp.float32),
        lax.psum(owned[10].astype(jnp.bfloat16), "dp").astype(jnp.float32),
        lax.psum(owned[11].astype(jnp.bfloat16), "dp").astype(jnp.float32),
        lax.psum(owned[12].astype(jnp.bfloat16), "dp").astype(jnp.float32),
        lax.psum(owned[13].astype(jnp.bfloat16), "dp").astype(jnp.float32),
        lax.psum(owned[14].astype(jnp.bfloat16), "dp").astype(jnp.float32),
    )
    return (
        block_output,
        input_grad.reshape(doc_count, seq_len, width),
        summed[0],
        summed[1],
        summed[2],
        summed[3],
        summed[4],
        summed[5],
        summed[6],
        summed[7],
        summed[8],
        summed[9],
        summed[10],
        summed[11],
        summed[12],
        summed[13],
        summed[14],
    )


def solution(mesh):
    in_specs = (
        P(("dp", "fsdp"), None, None),
        P(("dp", "fsdp")),
        P(("dp", "fsdp"), None, None),
        P("fsdp", None),
        P("fsdp"),
        P("fsdp", None),
        P("fsdp", None),
        P("fsdp"),
        P("fsdp", None),
        P("fsdp"),
        P("fsdp"),
        P("fsdp"),
        P("fsdp", None),
        P("fsdp"),
        P("fsdp", None),
        P("fsdp"),
        P("fsdp"),
        P("fsdp"),
    )
    out_specs = (
        P(("dp", "fsdp"), None, None),
        P(("dp", "fsdp"), None, None),
        P("fsdp", None),
        P("fsdp"),
        P("fsdp", None),
        P("fsdp", None),
        P("fsdp"),
        P("fsdp", None),
        P("fsdp"),
        P("fsdp"),
        P("fsdp"),
        P("fsdp", None),
        P("fsdp"),
        P("fsdp", None),
        P("fsdp"),
        P("fsdp"),
        P("fsdp"),
    )
    return jax.shard_map(
        on_device, mesh=mesh, in_specs=in_specs, out_specs=out_specs, check_vma=False
    )
```

profile of v0, /device:TPU:0, one launch (start us, length us, event | category | flops | bytes accessed | tf_op | source)
XLA Modules:
  0.0 681.5 jit_solution(11375898888319952286)
XLA Ops:
  14.5 30.3 %all-reduce.18 = (bf16[768]{0:T(1024)(128)(2,1)S(1)}, bf16[768]{0:T(1024)(128)(2,1)S(1)}, bf16[768]{0:T(1024)(128)(2,1)S(1)}, bf16[768]{0:T(1024)(128)(2,1)S(1)}...) all-reduce(bf16[768]{0:T(1024)(128)(2,1)S(1)} %dynamic-update-slice, ...), channel_id=1, replica_groups=mesh['dp'=4,'fsdp'=8] {'fsdp'}, use_global_device_ids=true, to_apply=%add | all-reduce | flops 6144 | bytes 24576
  45.5 13.0 %all-gather = bf16[8,1,384]{2,1,0:T(2,128)(2,1)S(1)} all-gather(bf16[1,1,384]{2,1,0:T(2,128)(2,1)S(1)} %reshape.181), channel_id=1, replica_groups=mesh['dp'=4,'fsdp'=8] {'fsdp'}, dimensions={0}, use_global_device_ids=true | all-gather | bytes 6912 | tf_op jit(solution)/shard_map/all_gather | solution.py:121
  58.6 2.0 add_convert_fusion
  61.0 2.3 convolution_convert_fusion.1
  63.6 19.9 %all-gather.8.cloned.1.call-done = bf16[768,768]{1,0:T(8,128)(2,1)} async-done(((bf16[96,768]{1,0:T(8,128)(2,1)}), bf16[768,768]{1,0:T(8,128)(2,1)}) %all-gather.8.cloned.1.call-update) | async-done | bytes 1179664 | tf_op jit(solution)/shard_map/all_gather | solution.py:114
  83.5 2.9 add_convert_fusion.1
  87.8 3.1 fusion
  90.9 2.6 exponential_reduce_fusion
  93.5 1.9 copy-done
  95.5 9.9 %fusion.1 = bf16[12,512,512]{1,2,0:T(8,128)(2,1)} fusion(f32[12,512,512]{1,2,0:T(8,128)} %copy-done, f32[12,512]{1,0:T(8,128)S(1)} %log_add_fusion, pred[512]{0:T(512)(128)(4,1)S(1)} %iota_compare_fusion), kind=kLoop, calls=%fused_computation.7 | loop fusion | flops 12582912 | bytes 18899456 | tf_op jit(solution)/shard_map/while/body/eval_jaxpr/convert_element_type | solution.py:46
  105.4 4.4 convolution_convert_fusion.3
  109.8 2.5 fusion.39
  113.8 46.7 %all-gather.16.cloned.1.call-done = bf16[768,3072]{1,0:T(8,128)(2,1)} async-done(((bf16[96,3072]{1,0:T(8,128)(2,1)}), bf16[768,3072]{1,0:T(8,128)(2,1)}) %all-gather.16.cloned.1.call-update) | async-done | bytes 4718608 | tf_op jit(solution)/shard_map/all_gather | solution.py:120
  160.4 8.5 %multiply_convert_fusion.1 = (bf16[512,3072]{1,0:T(8,128)(2,1)}, f32[512,3072]{1,0:T(8,128)}) fusion(f32[3072]{0:T(1024)S(1)} %bitcast.111, bf16[768,3072]{1,0:T(8,128)(2,1)} %all-gather.16.cloned.1.call-done, f32[512,768]{1,0:T(8,128)} %copy-done.15, f32[768]{0:T(1024)S(1)} %convert_element_type.234, f32[768]{0:T(1024)S(1)} %convert_element_type.233, ...), kind=kOutput, calls=%fused_computation.15 | convolution fusion | flops 2427322368 | bytes 15751168 | tf_op jit(solution)/shard_map/dot_general | solution.py:171
  169.0 43.5 %all-gather.18.cloned.1.call-done = bf16[3072,768]{1,0:T(8,128)(2,1)} async-done(((bf16[384,768]{1,0:T(8,128)(2,1)}), bf16[3072,768]{1,0:T(8,128)(2,1)}) %all-gather.18.cloned.1.call-update) | async-done | bytes 4718608 | tf_op jit(solution)/shard_map/all_gather | solution.py:122
  212.5 6.2 fusion.40
  222.4 4.9 convert_reduce_fusion
  227.4 3.1 multiply_reduce_fusion.1
  233.5 2.3 copy.65
  235.9 5.2 convert_reduce_fusion.3
  242.0 2.2 convolution_bitcast_fusion
  244.1 3.0 copy.80
  247.2 7.6 %multiply_reduce_fusion = (f32[12,512]{1,0:T(8,128)S(1)}, f32[12,512,512]{1,2,0:T(8,128)S(1)}) fusion(f32[12,512,512]{1,2,0:T(8,128)} %copy-done, f32[12,512]{1,0:T(8,128)S(1)} %log_add_fusion, pred[512]{0:T(512)(128)(4,1)S(1)} %iota_compare_fusion, bf16[512,12,64]{0,2,1:T(8,128)(2,1)} %bitcast.100, bf16[512,12,64]{0,2,1:T(8,128)(2,1)S(1)} %bitcast.96), kind=kOutput, calls=%fused_computation.1 | convolution fusion | flops 418375680 | bytes 26788352 | tf_op jit(solution)/shard_map/while/body/eval_jaxpr/qhd,khd->hqk/dot_general | solution.py:60
  254.8 7.2 %multiply_convert_fusion = bf16[12,512,512]{1,2,0:T(8,128)(2,1)S(1)} fusion(f32[12,512,512]{1,2,0:T(8,128)S(1)} %get-tuple-element.176, f32[12,512,512]{1,2,0:T(8,128)} %copy-done, f32[12,512]{1,0:T(8,128)S(1)} %get-tuple-element.175, f32[12,512]{1,0:T(8,128)S(1)} %log_add_fusion, pred[512]{0:T(512)(128)(4,1)S(1)} %iota_compare_fusion), kind=kLoop, calls=%fused_computation | loop fusion | flops 18874368 | bytes 31506944 | tf_op jit(solution)/shard_map/while/body/eval_jaxpr/convert_element_type | solution.py:64
  265.5 2.2 convolution_bitcast_fusion.2
  267.8 3.1 copy.76
  272.0 2.2 fusion.26
  275.4 4.8 multiply_convert_fusion.2
  281.1 2.2 convolution_bitcast_fusion.1
  283.3 3.1 copy.78
  287.8 7.2 %fusion.33 = f32[768,3072]{1,0:T(8,128)} fusion(bf16[512,3072]{1,0:T(8,128)(2,1)} %copy-done.41, f32[512,768]{1,0:T(8,128)S(1)} %copy-done.18, f32[768]{0:T(1024)S(1)} %convert_element_type.234, f32[768]{0:T(1024)S(1)} %convert_element_type.233, f32[512]{0:T(512)S(1)} %add_rsqrt_fusion.1, f32[512]{0:T(512)S(1)} %broadcast_multiply_fusion.5), kind=kOutput, calls=%fused_computation.91 | convolution fusion | flops 2417885184 | bytes 14166016 | tf_op jit(solution)/shard_map/tr,tc->rc/dot_general | solution.py:83
  296.4 8.2 %fusion.29 = f32[3072,768]{1,0:T(8,128)} fusion(bf16[512,3072]{1,0:T(8,128)(2,1)} %get-tuple-element.170, f32[512,768]{1,0:T(8,128)S(1)} %copy-done.14), kind=kOutput, calls=%fused_computation.87 | convolution fusion | flops 2416312320 | bytes 14155776 | tf_op jit(solution)/shard_map/tr,tc->rc/dot_general | solution.py:83
  304.7 1.8 copy.81
  306.5 13.8 %reduce-scatter.19.cloned.1.call-done = f32[96,768]{1,0:T(8,128)} async-done(((f32[768,768]{1,0:T(8,128)}), f32[96,768]{1,0:T(8,128)}) %reduce-scatter.19.cloned.1.call-update) | async-done | bytes 294928
  320.3 1.8 copy.77
  322.0 36.1 %reduce-scatter.13.cloned.1.call-done = f32[96,768]{1,0:T(8,128)} async-done(((f32[768,768]{1,0:T(8,128)}), f32[96,768]{1,0:T(8,128)}) %reduce-scatter.13.cloned.1.call-update) | async-done | bytes 294928 | tf_op jit(solution)/shard_map/reduce_scatter | solution.py:277
  359.8 36.0 %reduce-scatter.21.cloned.1.call-done = f32[96,768]{1,0:T(8,128)} async-done(((f32[768,768]{1,0:T(8,128)}), f32[96,768]{1,0:T(8,128)}) %reduce-scatter.21.cloned.1.call-update) | async-done | bytes 294928
  395.7 1.8 copy.79
  397.5 99.3 %reduce-scatter.15.cloned.1.call-done = f32[96,3072]{1,0:T(8,128)} async-done(((f32[768,3072]{1,0:T(8,128)}), f32[96,3072]{1,0:T(8,128)}) %reduce-scatter.15.cloned.1.call-update) | async-done | bytes 1179664 | tf_op jit(solution)/shard_map/reduce_scatter | solution.py:281
  496.8 2.1 convert_element_type.276
  499.0 97.9 %reduce-scatter.17.cloned.1.call-done = f32[384,768]{1,0:T(8,128)} async-done(((f32[3072,768]{1,0:T(8,128)}), f32[384,768]{1,0:T(8,128)}) %reduce-scatter.17.cloned.1.call-update) | async-done | bytes 1179664 | tf_op jit(solution)/shard_map/reduce_scatter | solution.py:283
  596.9 2.2 convert_element_type.281
  600.5 26.4 %all-reduce.17 = (bf16[768]{0:T(1024)(128)(2,1)S(1)}, bf16[768]{0:T(1024)(128)(2,1)S(1)}, bf16[768]{0:T(1024)(128)(2,1)S(1)}, bf16[768]{0:T(1024)(128)(2,1)S(1)}...) all-reduce(f32[768]{0:T(1024)S(1)} %reduce_sum.188, ...), channel_id=3, replica_groups=mesh['dp'=4,'fsdp'=8] {'fsdp'}, use_global_device_ids=true, to_apply=%region_14.15.clone | all-reduce | flops 9216 | bytes 55296
  627.6 10.0 %all-reduce.19 = (bf16[96]{0:T(256)(128)(2,1)S(1)}, bf16[96]{0:T(256)(128)(2,1)S(1)}, bf16[96]{0:T(256)(128)(2,1)S(1)}, bf16[96]{0:T(256)(128)(2,1)S(1)}, bf16[9...) all-reduce(bf16[96]{0:T(256)(128)(2,1)S(1)} %dynamic-slice.44, ...), channel_id=1, replica_groups=mesh['dp'=4,'fsdp'=8] {'dp'}, use_global_device_ids=true, to_apply=%region_15.16 | all-reduce | flops 1152 | bytes 4608 | tf_op jit(solution)/shard_map/psum | solution.py:290
  642.3 2.2 fusion.41
  646.1 2.1 add_bitcast_fusion
  648.1 20.0 %all-reduce.23.cloned.1.call-done = (bf16[96,768]{0,1:T(8,128)(2,1)}, bf16[96,768]{0,1:T(8,128)(2,1)}, bf16[96,768]{0,1:T(8,128)(2,1)}, bf16[96,768]{1,0:T(8,128...) async-done(((bf16[96,768]{0,1:T(8,128)(2,1)}, bf16[96,768]{0,1:T(8,128)(2,1)}, bf16[96,768]{0,1:T(8,128)(2,1)}, bf16[96,768]{1,0:T(8,128)(2,1)}, ...) | async-done | bytes 1769488 | tf_op jit(solution)/shard_map/psum | solution.py:289
  668.1 2.3 convert_element_type.277
  (194 shorter events, 40.2 us)
Async XLA Ops:
  7.2 4.1 copy-start.28
  7.2 5.4 copy-start.33
  7.2 5.6 copy-start.34
  7.2 5.8 copy-start.35
  7.2 6.1 copy-start.36
  7.2 6.3 copy-start.37
  7.3 6.5 copy-start.38
  7.3 6.7 copy-start.39
  7.3 7.0 %copy-start.40 = (bf16[96]{0:T(256)(128)(2,1)S(1)}, bf16[96]{0:T(256)(128)(2,1)}, u32[]{:S(2)}) copy-start(bf16[96]{0:T(256)(128)(2,1)} %param.35) | copy-start | bytes 580
  7.3 38.2 %copy-start.29 = (bf16[384]{0:T(512)(128)(2,1)S(1)}, bf16[384]{0:T(512)(128)(2,1)}, u32[]{:S(2)}) copy-start(bf16[384]{0:T(512)(128)(2,1)} %param.31) | copy-start | bytes 2308
  7.3 51.3 %copy-start.4 = (bf16[1,512,768]{2,1,0:T(8,128)(2,1)S(1)}, bf16[1,512,768]{2,1,0:T(8,128)(2,1)}, u32[]{:S(2)}) copy-start(bf16[1,512,768]{2,1,0:T(8,128)(2,1)} %param.18) | copy-start | bytes 2359300
  7.3 51.3 %all-gather.10.cloned.1.call-start = ((), (), s32[]{:S(2)}) async-start(), calls=%async_computation.7 | async-start | bytes 1327104 | tf_op jit(solution)/shard_map/all_gather | solution.py:111
  8.0 53.0 %all-gather.12.cloned.1.call-start = ((), (), s32[]{:S(2)}) async-start(), calls=%async_computation.8 | async-start | bytes 1327104 | tf_op jit(solution)/shard_map/all_gather | solution.py:113
  8.8 74.7 %all-gather.8.cloned.1.call-start = ((), (), s32[]{:S(2)}) async-start(), calls=%async_computation.6 | async-start | bytes 1327104 | tf_op jit(solution)/shard_map/all_gather | solution.py:114
  9.5 100.3 %all-gather.14.cloned.1.call-start = ((), (), s32[]{:S(2)}) async-start(), calls=%async_computation.9 | async-start | bytes 1327104 | tf_op jit(solution)/shard_map/all_gather | solution.py:116
  10.1 150.3 %all-gather.16.cloned.1.call-start = ((), (), s32[]{:S(2)}) async-start(), calls=%async_computation.10 | async-start | bytes 5308416 | tf_op jit(solution)/shard_map/all_gather | solution.py:120
  10.7 201.8 %all-gather.18.cloned.1.call-start = ((), (), s32[]{:S(2)}) async-start(), calls=%async_computation.11 | async-start | bytes 5308416 | tf_op jit(solution)/shard_map/all_gather | solution.py:122
  11.3 293.5 %reduce-scatter.23.cloned.1.call-start = ((), (), s32[]{:S(2)}) async-start(), calls=%async_computation.17 | async-start | bytes 2654208
  61.0 26.9 %copy-start.2 = (bf16[512,768]{0,1:T(8,128)(2,1)}, bf16[512,768]{0,1:T(8,128)(2,1)S(1)}, u32[]{:S(2)}) copy-start(bf16[512,768]{0,1:T(8,128)(2,1)S(1)} %copy.62) | copy-start | bytes 2359300
  90.9 4.5 copy-start
  109.8 2.5 copy-start.9
  160.4 52.0 %copy-start.16 = (f32[512,768]{1,0:T(8,128)S(1)}, f32[512,768]{1,0:T(8,128)}, u32[]{:S(2)}) copy-start(f32[512,768]{1,0:T(8,128)} %copy-done.15) | copy-start | bytes 4718596
  212.5 9.9 %copy-start.42 = (f32[512,3072]{1,0:T(8,128)S(1)}, f32[512,3072]{1,0:T(8,128)}, u32[]{:S(2)}) copy-start(f32[512,3072]{1,0:T(8,128)} %get-tuple-element.171) | copy-start | bytes 18874372
  219.8 2.6 copy-start.30
  220.7 6.6 slice-start
  222.4 5.0 copy-start.13
  222.4 5.0 slice-start.1
  227.3 3.2 copy-start.41
  227.4 3.2 copy-start.17
  235.9 6.1 copy-start.5
  247.2 73.1 %reduce-scatter.19.cloned.1.call-start = ((), (), s32[]{:S(2)}) async-start(), calls=%async_computation.15 | async-start | bytes 2654208
  262.0 2.7 copy-start.1
  262.0 3.5 copy-start.6
  270.9 87.2 %reduce-scatter.13.cloned.1.call-start = ((), (), s32[]{:S(2)}) async-start(), calls=%async_computation.12 | async-start | bytes 2654208 | tf_op jit(solution)/shard_map/reduce_scatter | solution.py:277
  274.3 121.5 %reduce-scatter.21.cloned.1.call-start = ((), (), s32[]{:S(2)}) async-start(), calls=%async_computation.16 | async-start | bytes 2654208
  286.4 210.4 %reduce-scatter.15.cloned.1.call-start = ((), (), s32[]{:S(2)}) async-start(), calls=%async_computation.13 | async-start | bytes 10616832 | tf_op jit(solution)/shard_map/reduce_scatter | solution.py:281
  295.0 1.4 copy-start.14
  295.0 301.9 %reduce-scatter.17.cloned.1.call-start = ((), (), s32[]{:S(2)}) async-start(), calls=%async_computation.14 | async-start | bytes 10616832 | tf_op jit(solution)/shard_map/reduce_scatter | solution.py:283
  304.7 363.4 %all-reduce.23.cloned.1.call-start = ((), (), s32[]{:S(2)}) async-start(), calls=%async_computation.18 | async-start | bytes 3833856 | tf_op jit(solution)/shard_map/psum | solution.py:289
  499.0 143.3 %copy-start.12 = (bf16[12,64,512]{2,1,0:T(8,128)(2,1)S(1)}, bf16[12,64,512]{2,1,0:T(8,128)(2,1)}, u32[]{:S(2)}) copy-start(bf16[12,64,512]{2,1,0:T(8,128)(2,1)} %copy-done.11) | copy-start | bytes 2359300
  642.3 2.2 copy-start.21
  642.3 2.3 copy-start.31
  644.6 1.5 copy-start.22
  668.1 2.3 copy-start.23
  668.1 3.4 copy-start.27
  668.1 4.1 copy-start.26
  670.4 2.7 copy-start.25
  670.4 3.5 copy-start.24
  (10 other events, 11.0 us)
Sparse Core Ops, SparseCore 0:
  9.8 25.5 all-gather.9
  37.0 22.5 all-gather.11
  61.2 22.1 all-gather.7
  85.0 22.4 all-gather.13
  108.9 51.4 all-gather.15
  161.9 50.5 all-gather.17
  247.3 35.0 reduce-scatter.22
  284.7 35.5 reduce-scatter.18
  322.6 35.4 reduce-scatter.12
  360.3 35.4 reduce-scatter.20
  398.1 98.7 reduce-scatter.14
  499.0 97.8 reduce-scatter.16
  601.3 66.7 all-reduce.22
where the time goes:
time: 686 us; the launch traced here: 682 us
  waiting for transfers between devices  417 us (61%)
  matrix products  89.9 us (13%)
  blocking collectives  79.7 us (12%)
  local copies, waits for them, and re-layouts  38.8 us (6%)
  other arithmetic  38.1 us (6%)
  between operations  17.4 us (3%)
    reduce_scatter x1, waiting for transfers between devices, on_device(): lax.psum_scatter(local_grads[9], 'fsdp', scatter_dimension=0, tiled=True)  99.3 us
    reduce_scatter x1, waiting for transfers between devices, on_device(): lax.psum_scatter(local_grads[11], 'fsdp', scatter_dimension=0, tiled=True)  97.9 us
    unnamed x2, blocking collectives  56.7 us
    unnamed x16, waiting for transfers between devices  53.5 us
    all_gather x1, waiting for transfers between devices, on_device(): lax.all_gather(inner_weight, 'fsdp', axis=0, tiled=True)  46.7 us
    all_gather x1, waiting for transfers between devices, on_device(): lax.all_gather(outer_weight, 'fsdp', axis=0, tiled=True)  43.5 us
    reduce_scatter x1, waiting for transfers between devices, on_device(): lax.psum_scatter(local_grads[5], 'fsdp', scatter_dimension=0, tiled=True)  36.1 us
    unnamed x126, local copies, waits for them, and re-layouts  34.3 us
  transfers between devices with their start and end apart: 13, of which 9 were waited for; matrix products, arithmetic and copies ran while one was open for 16% of the time, Pallas kernels for 0%

commit v1 on v0

--- a/solution.py
+++ b/solution.py
@@ -9,6 +9,18 @@
 masked_score = -1e30
 root_half = math.sqrt(0.5)
 inv_root_two_pi = 1.0 / math.sqrt(2.0 * math.pi)
+
+
+def collect(x, axis, dim):
+    ways, here = (lax.axis_size(axis), lax.axis_index(axis))
+    grown, reach = (x, 1)
+    while reach < ways:
+        theirs = lax.ppermute(grown, axis, [(d, d ^ reach) for d in range(ways)])
+        mine_first = jnp.concatenate([grown, theirs], axis=dim)
+        theirs_first = jnp.concatenate([theirs, grown], axis=dim)
+        grown = jnp.where(here & reach == 0, mine_first, theirs_first)
+        reach = 2 * reach
+    return grown
 
 
 def normalize(values):
@@ -119,7 +131,7 @@
         lax.all_gather(first_shift, "fsdp", axis=0, tiled=True),
         lax.all_gather(inner_weight, "fsdp", axis=0, tiled=True),
         lax.all_gather(inner_bias, "fsdp", axis=0, tiled=True),
-        lax.all_gather(outer_weight, "fsdp", axis=0, tiled=True),
+        collect(outer_weight, "fsdp", 0),
         lax.all_gather(outer_bias, "fsdp", axis=0, tiled=True),
         lax.all_gather(second_gain, "fsdp", axis=0, tiled=True),
         lax.all_gather(second_shift, "fsdp", axis=0, tiled=True),

time: 686 us -> 781 us (1.14)
  waiting for transfers between devices: 417 us -> 474 us
  blocking collectives: 79.7 us -> 105 us
    all_gather x1, waiting for transfers between devices: 46.7 us -> 93.5 us  [on_device(): lax.all_gather(inner_weight, 'fsdp', axis=0, tiled=True)]
    all_gather x1, waiting for transfers between devices: 0.02 us -> 39.5 us  [on_device(): lax.all_gather(output_weight, 'fsdp', axis=0, tiled=True)]
    unnamed x2, blocking collectives: 56.7 us -> 82.1 us
    all_gather x1, waiting for transfers between devices: 19.9 us -> 0.01 us  [on_device(): lax.all_gather(value_weight, 'fsdp', axis=0, tiled=True)]
    all_gather x1, waiting for transfers between devices: 43.5 us -> 33.1 us  [on_device(): lax.all_gather(outer_weight, 'fsdp', axis=0, tiled=True)]
    unnamed x126 -> x122, local copies, waits for them, and re-layouts: 34.3 us -> 34.4 us
  transfers between devices with their start and end apart: 13 -> 16, of which waited for: 9 -> 10; matrix products, arithmetic and copies ran while one was open for 16% -> 16% of each run, Pallas kernels for 0% -> 0%
where the time goes in v1:
time: 781 us; the launch traced here: 776 us
  waiting for transfers between devices  474 us (61%)
  blocking collectives  105 us (13%)
  matrix products  95.2 us (12%)
  other arithmetic  41.7 us (5%)
  local copies, waits for them, and re-layouts  37.6 us (5%)
  between operations  17.4 us (2%)
    reduce_scatter x1, waiting for transfers between devices, on_device(): lax.psum_scatter(local_grads[9], 'fsdp', scatter_dimension=0, tiled=True)  99.4 us
    reduce_scatter x1, waiting for transfers between devices, on_device(): lax.psum_scatter(local_grads[11], 'fsdp', scatter_dimension=0, tiled=True)  97.9 us
    all_gather x1, waiting for transfers between devices, on_device(): lax.all_gather(inner_weight, 'fsdp', axis=0, tiled=True)  93.5 us
    unnamed x2, blocking collectives  82.1 us
    unnamed x16, waiting for transfers between devices  53 us
    all_gather x1, waiting for transfers between devices, on_device(): lax.all_gather(output_weight, 'fsdp', axis=0, tiled=True)  39.5 us
    reduce_scatter x1, waiting for transfers between devices, on_device(): lax.psum_scatter(local_grads[5], 'fsdp', scatter_dimension=0, tiled=True)  36.1 us
    unnamed x122, local copies, waits for them, and re-layouts  34.4 us
  transfers between devices with their start and end apart: 16, of which 10 were waited for; matrix products, arithmetic and copies ran while one was open for 16% of the time, Pallas kernels for 0%

profile of v1, /device:TPU:0, one launch (start us, length us, event | category | flops | bytes accessed | tf_op | source)
XLA Modules:
  0.0 776.0 jit_solution(16158537936012075230)
XLA Ops:
  11.3 1.8 collective-permute-done
  13.6 3.0 collective-permute-start.1
  19.8 55.7 %all-reduce.18 = (bf16[768]{0:T(1024)(128)(2,1)S(1)}, bf16[768]{0:T(1024)(128)(2,1)S(1)}, bf16[768]{0:T(1024)(128)(2,1)S(1)}, bf16[768]{0:T(1024)(128)(2,1)S(1)}...) all-reduce(bf16[768]{0:T(1024)(128)(2,1)S(1)} %dynamic-update-slice, ...), channel_id=1, replica_groups=mesh['dp'=4,'fsdp'=8] {'fsdp'}, use_global_device_ids=true, to_apply=%add | all-reduce | flops 6144 | bytes 24576
  76.2 12.7 %all-gather = bf16[8,1,384]{2,1,0:T(2,128)(2,1)S(1)} all-gather(bf16[1,1,384]{2,1,0:T(2,128)(2,1)S(1)} %reshape.181), channel_id=1, replica_groups=mesh['dp'=4,'fsdp'=8] {'fsdp'}, dimensions={0}, use_global_device_ids=true | all-gather | bytes 6912 | tf_op jit(solution)/shard_map/all_gather | solution.py:133
  89.0 3.3 maximum_select_fusion.2
  93.3 2.0 add_convert_fusion
  95.7 2.3 convolution_convert_fusion.1
  98.3 3.1 fusion
  101.4 2.6 exponential_reduce_fusion
  104.0 1.9 copy-done
  105.9 9.8 %fusion.1 = bf16[12,512,512]{1,2,0:T(8,128)(2,1)} fusion(f32[12,512,512]{1,2,0:T(8,128)} %copy-done, f32[12,512]{1,0:T(8,128)S(1)} %log_add_fusion, pred[512]{0:T(512)(128)(4,1)S(1)} %iota_compare_fusion), kind=kLoop, calls=%fused_computation.7 | loop fusion | flops 12582912 | bytes 18899456 | tf_op jit(solution)/shard_map/while/body/eval_jaxpr/convert_element_type | solution.py:58
  115.7 2.0 add_convert_fusion.1
  118.0 4.1 convolution_convert_fusion.3
  122.2 39.5 %all-gather.14.cloned.1.call-done = bf16[768,768]{1,0:T(8,128)(2,1)} async-done(((bf16[96,768]{1,0:T(8,128)(2,1)}), bf16[768,768]{1,0:T(8,128)(2,1)}) %all-gather.14.cloned.1.call-update) | async-done | bytes 1179664 | tf_op jit(solution)/shard_map/all_gather | solution.py:128
  161.7 2.2 fusion.47
  165.3 93.5 %all-gather.16.cloned.1.call-done = bf16[768,3072]{1,0:T(8,128)(2,1)} async-done(((bf16[96,3072]{1,0:T(8,128)(2,1)}), bf16[768,3072]{1,0:T(8,128)(2,1)}) %all-gather.16.cloned.1.call-update) | async-done | bytes 4718608 | tf_op jit(solution)/shard_map/all_gather | solution.py:132
  258.8 7.6 multiply_convert_fusion.1
  266.3 7.7 fusion.48
  277.7 33.1 %all-gather.18.cloned.1.call-done = bf16[3072,768]{1,0:T(8,128)(2,1)} async-done(((bf16[384,768]{1,0:T(8,128)(2,1)}), bf16[3072,768]{1,0:T(8,128)(2,1)}) %all-gather.18.cloned.1.call-update) | async-done | bytes 4718608 | tf_op jit(solution)/shard_map/all_gather | solution.py:215
  310.8 7.7 convert_reduce_fusion
  318.5 6.6 multiply_reduce_fusion.1
  328.1 2.3 copy.65
  330.4 5.2 convert_reduce_fusion.3
  336.5 2.2 convolution_bitcast_fusion
  338.6 3.0 copy.80
  341.8 7.6 multiply_reduce_fusion
  349.4 7.2 multiply_convert_fusion
  360.0 2.2 convolution_bitcast_fusion.2
  362.3 3.1 copy.76
  366.5 2.2 fusion.34
  369.9 4.8 multiply_convert_fusion.2
  375.6 2.2 convolution_bitcast_fusion.1
  377.8 3.0 copy.78
  382.3 7.2 fusion.41
  390.9 8.2 %fusion.37 = f32[3072,768]{1,0:T(8,128)} fusion(bf16[512,3072]{1,0:T(8,128)(2,1)} %copy-done.19, f32[512,768]{1,0:T(8,128)S(1)} %copy-done.14), kind=kOutput, calls=%fused_computation.98 | convolution fusion | flops 2416312320 | bytes 14155776 | tf_op jit(solution)/shard_map/tr,tc->rc/dot_general | solution.py:95
  401.0 13.7 %reduce-scatter.19.cloned.1.call-done = f32[96,768]{1,0:T(8,128)} async-done(((f32[768,768]{1,0:T(8,128)}), f32[96,768]{1,0:T(8,128)}) %reduce-scatter.19.cloned.1.call-update) | async-done | bytes 294928
  416.5 36.1 %reduce-scatter.13.cloned.1.call-done = f32[96,768]{1,0:T(8,128)} async-done(((f32[768,768]{1,0:T(8,128)}), f32[96,768]{1,0:T(8,128)}) %reduce-scatter.13.cloned.1.call-update) | async-done | bytes 294928 | tf_op jit(solution)/shard_map/reduce_scatter | solution.py:289
  454.2 36.0 %reduce-scatter.21.cloned.1.call-done = f32[96,768]{1,0:T(8,128)} async-done(((f32[768,768]{1,0:T(8,128)}), f32[96,768]{1,0:T(8,128)}) %reduce-scatter.21.cloned.1.call-update) | async-done | bytes 294928
  492.0 99.4 %reduce-scatter.15.cloned.1.call-done = f32[96,3072]{1,0:T(8,128)} async-done(((f32[768,3072]{1,0:T(8,128)}), f32[96,3072]{1,0:T(8,128)}) %reduce-scatter.15.cloned.1.call-update) | async-done | bytes 1179664 | tf_op jit(solution)/shard_map/reduce_scatter | solution.py:293
  591.4 2.2 convert_element_type.276
  593.5 97.9 %reduce-scatter.17.cloned.1.call-done = f32[384,768]{1,0:T(8,128)} async-done(((f32[3072,768]{1,0:T(8,128)}), f32[384,768]{1,0:T(8,128)}) %reduce-scatter.17.cloned.1.call-update) | async-done | bytes 1179664 | tf_op jit(solution)/shard_map/reduce_scatter | solution.py:295
  691.4 2.2 convert_element_type.281
  695.1 26.4 %all-reduce.17 = (bf16[768]{0:T(1024)(128)(2,1)S(1)}, bf16[768]{0:T(1024)(128)(2,1)S(1)}, bf16[768]{0:T(1024)(128)(2,1)S(1)}, bf16[768]{0:T(1024)(128)(2,1)S(1)}...) all-reduce(f32[768]{0:T(1024)S(1)} %reduce_sum.188, ...), channel_id=3, replica_groups=mesh['dp'=4,'fsdp'=8] {'fsdp'}, use_global_device_ids=true, to_apply=%region_14.15.clone | all-reduce | flops 9216 | bytes 55296
  722.2 10.0 %all-reduce.19 = (bf16[96]{0:T(256)(128)(2,1)S(1)}, bf16[96]{0:T(256)(128)(2,1)S(1)}, bf16[96]{0:T(256)(128)(2,1)S(1)}, bf16[96]{0:T(256)(128)(2,1)S(1)}, bf16[9...) all-reduce(bf16[96]{0:T(256)(128)(2,1)S(1)} %dynamic-slice.44, ...), channel_id=1, replica_groups=mesh['dp'=4,'fsdp'=8] {'dp'}, use_global_device_ids=true, to_apply=%region_15.16 | all-reduce | flops 1152 | bytes 4608 | tf_op jit(solution)/shard_map/psum | solution.py:302
  736.8 2.2 fusion.49
  740.6 2.1 add_bitcast_fusion
  742.7 20.0 %all-reduce.23.cloned.1.call-done = (bf16[96,768]{0,1:T(8,128)(2,1)}, bf16[96,768]{0,1:T(8,128)(2,1)}, bf16[96,768]{0,1:T(8,128)(2,1)}, bf16[96,768]{1,0:T(8,128...) async-done(((bf16[96,768]{0,1:T(8,128)(2,1)}, bf16[96,768]{0,1:T(8,128)(2,1)}, bf16[96,768]{0,1:T(8,128)(2,1)}, bf16[96,768]{1,0:T(8,128)(2,1)}, ...) | async-done | bytes 1769488 | tf_op jit(solution)/shard_map/psum | solution.py:301
  762.6 2.3 convert_element_type.277
  (197 shorter events, 45.7 us)
Async XLA Ops:
  7.2 5.9 copy-start.23
  7.2 86.1 %all-gather.10.cloned.1.call-start = ((), (), s32[]{:S(2)}) async-start(), calls=%async_computation.7 | async-start | bytes 1327104 | tf_op jit(solution)/shard_map/all_gather | solution.py:123
  7.9 87.7 %all-gather.12.cloned.1.call-start = ((), (), s32[]{:S(2)}) async-start(), calls=%async_computation.8 | async-start | bytes 1327104 | tf_op jit(solution)/shard_map/all_gather | solution.py:125
  8.7 107.0 %all-gather.8.cloned.1.call-start = ((), (), s32[]{:S(2)}) async-start(), calls=%async_computation.6 | async-start | bytes 1327104 | tf_op jit(solution)/shard_map/all_gather | solution.py:126
  9.4 152.2 %all-gather.14.cloned.1.call-start = ((), (), s32[]{:S(2)}) async-start(), calls=%async_computation.9 | async-start | bytes 1327104 | tf_op jit(solution)/shard_map/all_gather | solution.py:128
  10.0 248.8 %all-gather.16.cloned.1.call-start = ((), (), s32[]{:S(2)}) async-start(), calls=%async_computation.10 | async-start | bytes 5308416 | tf_op jit(solution)/shard_map/all_gather | solution.py:132
  10.6 6.1 copy-start.30
  10.6 7.3 copy-start.34
  10.6 7.6 copy-start.35
  10.6 7.8 %copy-start.36 = (bf16[96]{0:T(256)(128)(2,1)S(1)}, bf16[96]{0:T(256)(128)(2,1)}, u32[]{:S(2)}) copy-start(bf16[96]{0:T(256)(128)(2,1)} %param.27) | copy-start | bytes 580
  10.6 8.0 %copy-start.37 = (bf16[96]{0:T(256)(128)(2,1)S(1)}, bf16[96]{0:T(256)(128)(2,1)}, u32[]{:S(2)}) copy-start(bf16[96]{0:T(256)(128)(2,1)} %param.28) | copy-start | bytes 580
  10.6 8.2 %copy-start.38 = (bf16[96]{0:T(256)(128)(2,1)S(1)}, bf16[96]{0:T(256)(128)(2,1)}, u32[]{:S(2)}) copy-start(bf16[96]{0:T(256)(128)(2,1)} %param.29) | copy-start | bytes 580
  10.6 8.5 %copy-start.39 = (bf16[96]{0:T(256)(128)(2,1)S(1)}, bf16[96]{0:T(256)(128)(2,1)}, u32[]{:S(2)}) copy-start(bf16[96]{0:T(256)(128)(2,1)} %param.33) | copy-start | bytes 580
  10.7 8.7 %copy-start.40 = (bf16[96]{0:T(256)(128)(2,1)S(1)}, bf16[96]{0:T(256)(128)(2,1)}, u32[]{:S(2)}) copy-start(bf16[96]{0:T(256)(128)(2,1)} %param.34) | copy-start | bytes 580
  10.7 8.9 %copy-start.41 = (bf16[96]{0:T(256)(128)(2,1)S(1)}, bf16[96]{0:T(256)(128)(2,1)}, u32[]{:S(2)}) copy-start(bf16[96]{0:T(256)(128)(2,1)} %param.35) | copy-start | bytes 580
  10.7 65.5 %copy-start.31 = (bf16[384]{0:T(512)(128)(2,1)S(1)}, bf16[384]{0:T(512)(128)(2,1)}, u32[]{:S(2)}) copy-start(bf16[384]{0:T(512)(128)(2,1)} %param.31) | copy-start | bytes 2308
  10.7 300.1 %all-gather.18.cloned.1.call-start = ((), (), s32[]{:S(2)}) async-start(), calls=%async_computation.11 | async-start | bytes 5308416 | tf_op jit(solution)/shard_map/all_gather | solution.py:215
  10.7 2.4 collective-permute-start
  13.6 75.5 %collective-permute-start.1 = (bf16[768,768]{1,0:T(8,128)(2,1)S(1)}, bf16[768,768]{1,0:T(8,128)(2,1)}, u32[]{:S(2)}, u32[]{:S(2)}) collective-permute-start(bf16[768,768]{1,0:T(8,128)(2,1)S(1)} %maximum_select_fusion.5), channel_id=1, source_target_pairs={{0,2},{1,3},{2,0},{3,1},{4,6},{5,7},{6,4},{7,5},{8,10},{9,11},{10,... | collective-permute-start | bytes 3538952 | tf_op jit(solution)/shard_map/ppermute | solution.py:18
  16.6 382.7 %reduce-scatter.23.cloned.1.call-start = ((), (), s32[]{:S(2)}) async-start(), calls=%async_computation.17 | async-start | bytes 2654208
  89.0 4.3 copy-start.4
  92.3 174.1 %collective-permute-start.2 = (bf16[1536,768]{1,0:T(8,128)(2,1)}, bf16[1536,768]{1,0:T(8,128)(2,1)}, u32[]{:S(2)}, u32[]{:S(2)}) collective-permute-start(bf16[1536,768]{1,0:T(8,128)(2,1)} %maximum_select_fusion.2), channel_id=1, source_target_pairs={{0,4},{1,5},{2,6},{3,7},{4,0},{5,1},{6,2},{7,3},{8,12},{9,13},{10,... | collective-permute-start | bytes 7077896 | tf_op jit(solution)/shard_map/ppermute | solution.py:18
  95.6 2.6 copy-start.2
  101.4 4.5 copy-start
  122.2 41.7 %copy-start.9 = (bf16[12,64,512]{2,1,0:T(8,128)(2,1)}, bf16[12,64,512]{2,1,0:T(8,128)(2,1)S(1)}, u32[]{:S(2)}) copy-start(bf16[12,64,512]{2,1,0:T(8,128)(2,1)S(1)} %convolution_convert_fusion.3) | copy-start | bytes 2359300
  258.8 7.6 copy-start.16
  266.3 7.7 copy-start.19
  277.7 40.7 %copy-start.13 = (f32[512,768]{1,0:T(8,128)}, f32[512,768]{1,0:T(8,128)S(1)}, u32[]{:S(2)}) copy-start(f32[512,768]{1,0:T(8,128)S(1)} %get-tuple-element.160) | copy-start | bytes 4718596
  310.8 7.7 copy-start.17
  318.5 6.6 copy-start.42
  330.4 6.1 copy-start.5
  341.7 73.0 %reduce-scatter.19.cloned.1.call-start = ((), (), s32[]{:S(2)}) async-start(), calls=%async_computation.15 | async-start | bytes 2654208
  356.5 2.6 copy-start.1
  356.5 3.5 copy-start.6
  365.4 87.1 %reduce-scatter.13.cloned.1.call-start = ((), (), s32[]{:S(2)}) async-start(), calls=%async_computation.12 | async-start | bytes 2654208 | tf_op jit(solution)/shard_map/reduce_scatter | solution.py:289
  368.8 121.4 %reduce-scatter.21.cloned.1.call-start = ((), (), s32[]{:S(2)}) async-start(), calls=%async_computation.16 | async-start | bytes 2654208
  380.9 210.5 %reduce-scatter.15.cloned.1.call-start = ((), (), s32[]{:S(2)}) async-start(), calls=%async_computation.13 | async-start | bytes 10616832 | tf_op jit(solution)/shard_map/reduce_scatter | solution.py:293
  389.5 301.9 %reduce-scatter.17.cloned.1.call-start = ((), (), s32[]{:S(2)}) async-start(), calls=%async_computation.14 | async-start | bytes 10616832 | tf_op jit(solution)/shard_map/reduce_scatter | solution.py:295
  399.2 363.5 %all-reduce.23.cloned.1.call-start = ((), (), s32[]{:S(2)}) async-start(), calls=%async_computation.18 | async-start | bytes 3833856 | tf_op jit(solution)/shard_map/psum | solution.py:301
  593.5 143.3 %copy-start.12 = (bf16[12,64,512]{2,1,0:T(8,128)(2,1)S(1)}, bf16[12,64,512]{2,1,0:T(8,128)(2,1)}, u32[]{:S(2)}) copy-start(bf16[12,64,512]{2,1,0:T(8,128)(2,1)} %copy-done.11) | copy-start | bytes 2359300
  736.8 2.2 copy-start.22
  736.8 2.3 copy-start.32
  739.1 1.5 copy-start.24
  762.6 2.3 copy-start.25
  762.6 3.4 copy-start.29
  762.6 4.1 copy-start.28
  764.9 2.7 copy-start.27
  764.9 3.5 copy-start.26
  (11 other events, 12.5 us)
Sparse Core Ops, SparseCore 0:
  9.7 31.6 all-gather.9
  43.0 24.7 all-gather.11
  69.4 22.1 all-gather.7
  93.2 68.4 all-gather.13
  163.1 95.5 all-gather.15
  260.3 50.5 all-gather.17
  341.8 35.3 reduce-scatter.22
  379.6 35.1 reduce-scatter.18
  417.0 35.4 reduce-scatter.12
  454.7 35.4 reduce-scatter.20
  492.6 98.7 reduce-scatter.14
  593.5 97.8 reduce-scatter.16
  695.9 66.7 all-reduce.22
